TPU v7x, 128 devices: a whole 4x4x4 slice. The times are simulated.
128 devices in a mesh: grp: 16 (over z, x), reg: 8 (over y, core).
Axes of the slice: x: 4, y: 4, z: 4, core: 2. Of those that a mesh axis runs over, the one named last changes fastest.
Arguments:
- orbitals: bfloat16 [8, 16, 512, 1024], P('reg', 'grp'), may hold values from -6 to 6
- occupied: bfloat16 [8, 16, 8, 512], P('reg', 'grp'), may hold values from -0.59765625 to 0.59765625
- panel_index: int32 [128], replicated, may hold values from 0 to 1023, as said below
- screening: bfloat16 [896, 512, 512], P(('grp', 'reg')), may hold values from -0.25 to 0.25
- block_region: int32 [896, 1], P(('grp', 'reg')), may hold values from 0 to 7; in each aligned block of 7 rows (0 to 6, 7 to 13, ...) at most 2 rows name the same one
- block_row: int32 [896], P(('grp', 'reg')), may hold values from 0 to 15
- block_col: int32 [896], P(('grp', 'reg')), may hold values from 0 to 15
Outputs:
- sigma: float32 [8, 128, 128], P('reg')
Inputs may be any that keep to these rules, and one draw needn't show every extreme that they name: `panel_index`: the 128 indices are distinct. Among the 7 blocks of one device (aligned rows of block_region), at most 2 name the same region.
All inputs are finite; a program needn't handle non-finite values.
Results may differ from a plain program's by a relative error of at most 0.0054.
Values may be sent and summed in bfloat16 or wider, within the bound.
A program may use at most 192 MiB of HBM per device.

v0:
```python
import jax
import jax.numpy as jnp
from jax import lax
from jax.sharding import PartitionSpec as P

CAP = 2


def form_pairs(orbital_rows, occupied_rows):
    pairs = orbital_rows[..., :, None, :].astype(jnp.float32) * jnp.swapaxes(occupied_rows, -1, -2)[
        ..., None
    ].astype(jnp.float32)
    return pairs.astype(jnp.bfloat16)


def shards(orbitals, occupied, panel_index, screening, block_region, block_row, block_col):
    regions = lax.axis_size("reg")
    panel_orbs = jnp.take(orbitals[0], panel_index, axis=2)
    occ_rows = occupied[0]
    grid_points = screening.shape[1]
    panel_width = panel_orbs.shape[2]
    occ_count = occ_rows.shape[1]
    held_count = screening.shape[0]
    slot_count = regions * CAP
    destination = block_region[:, 0]
    membership = (destination[:, None] == jnp.arange(regions, dtype=jnp.int32)[None, :]).astype(
        jnp.int32
    )
    earlier = jnp.cumsum(membership, axis=0) - membership
    slot_of = destination * CAP + jnp.sum(earlier * membership, axis=1)
    matched = (slot_of[None, :] == jnp.arange(slot_count, dtype=jnp.int32)[:, None]).astype(
        jnp.int32
    )
    filled = jnp.sum(matched, axis=1)
    source = jnp.sum(matched * jnp.arange(held_count, dtype=jnp.int32)[None, :], axis=1)
    outgoing = jnp.take(screening, source, axis=0) * filled[:, None, None].astype(jnp.bfloat16)
    labels = jnp.stack(
        [jnp.take(block_row, source) * filled, jnp.take(block_col, source) * filled, filled], axis=1
    )
    gathered = lax.all_gather(form_pairs(panel_orbs, occ_rows), "grp", axis=0, tiled=True)

    def select_pairs(indices):
        return jnp.take(gathered, indices, axis=0)

    incoming, arrived = (
        lax.all_to_all(
            outgoing.reshape(regions, CAP, grid_points, grid_points),
            "reg",
            split_axis=0,
            concat_axis=0,
            tiled=True,
        ),
        lax.all_to_all(
            labels.reshape(regions, CAP, 3), "reg", split_axis=0, concat_axis=0, tiled=True
        ),
    )
    incoming = incoming.reshape(slot_count, grid_points, grid_points)
    arrived = arrived.reshape(slot_count, 3)
    col_pairs = select_pairs(arrived[:, 1]).reshape(
        slot_count, grid_points, occ_count * panel_width
    )
    screened = jnp.einsum(
        "spq,sqc->spc", incoming, col_pairs, preferred_element_type=jnp.float32
    ).astype(jnp.bfloat16)
    row_pairs = select_pairs(arrived[:, 0]).reshape(
        slot_count, grid_points * occ_count, panel_width
    )
    partial_sigma = jnp.einsum(
        "sri,srj->ij",
        row_pairs,
        screened.reshape(slot_count, grid_points * occ_count, panel_width),
        preferred_element_type=jnp.float32,
    )
    sigma = lax.psum(partial_sigma, "grp")
    return sigma[None]


def solution(mesh):
    in_specs = (
        P("reg", "grp", None, None),
        P("reg", "grp", None, None),
        P(),
        P(("grp", "reg"), None, None),
        P(("grp", "reg"), None),
        P(("grp", "reg")),
        P(("grp", "reg")),
    )
    out_specs = P("reg", None, None)
    return jax.shard_map(shards, mesh=mesh, in_specs=in_specs, out_specs=out_specs, check_vma=False)
```

profile of v0, /device:TPU:0, one launch (start us, length us, event | category | flops | bytes accessed | tf_op | source)
XLA Modules:
  0.0 339.5 jit_solution(4951172310689396512)
XLA Ops:
  6.5 0.7 compare_and_fusion.4
  7.2 0.7 compare_select_fusion.5
  7.9 0.7 convert_bitcast_fusion.1
  8.6 0.1 copy.28
  8.7 1.5 copy.26
  10.2 0.8 gather_fusion
  11.1 0.1 convert_bitcast_fusion
  11.2 0.1 copy.27
  11.3 1.6 multiply_convert_fusion
  12.9 0.7 fusion.8
  13.6 0.8 select_reduce_fusion.1
  14.5 0.7 multiply_add_fusion
  15.1 0.1 convert_reduce_fusion
  15.2 0.7 gather_fusion.3
  15.9 1.3 gather_fusion.2
  17.5 0.7 copy.24
  18.2 4.6 %all-to-all-start = ((s32[8,2,3]{2,1,0:T(2,128)}), s32[8,2,3]{2,1,0:T(2,128)S(1)}, u32[]{:S(2)}, u32[]{:S(2)}) async-start(s32[8,2,3]{2,1,0:T(2,128)} %copy.24), calls=%async_computation | async-start | bytes 16384 | tf_op jit(solution)/shard_map/all_to_all | solution.py:53
  22.9 0.1 convert_element_type.65
  23.0 6.9 %gather_fusion.1 = bf16[16,512,512]{2,1,0:T(8,128)(2,1)} fusion(bf16[7,512,512]{2,1,0:T(8,128)(2,1)} %param.14, s32[1024]{0:T(1024)S(1)} %pad_clamp_fusion.1), kind=kCustom, calls=%fused_computation.5 | custom fusion | bytes 16777280 | tf_op jit(solution)/shard_map/jit(_take)/gather | solution.py:36
  29.9 7.4 %select_multiply_fusion = bf16[8,2,512,512]{3,2,1,0:T(8,128)(2,1)} fusion(bf16[8,2,512,512]{3,2,1,0:T(8,128)(2,1)} %bitcast.40, pred[8,2]{1,0:T(8,128)(4,1)S(1)} %compare_and_fusion, bf16[8,2]{1,0:T(8,128)(2,1)S(1)} %convert_element_type.65), kind=kLoop, calls=%fused_computation.13 | loop fusion | flops 8388608 | bytes 16777264 | tf_op jit(solution)/shard_map/mul | solution.py:36
  37.4 5.0 %all-to-all-start.1 = ((bf16[8,2,512,512]{3,2,1,0:T(8,128)(2,1)}), bf16[8,2,512,512]{3,2,1,0:T(8,128)(2,1)}, u32[]{:S(2)}, u32[]{:S(2)}) async-start(bf16[8,2,512,512]{3,2,1,0:T(8,128)(2,1)} %select_multiply_fusion), calls=%async_computation.1 | async-start | bytes 16777216 | tf_op jit(solution)/shard_map/all_to_all | solution.py:46
  42.3 0.2 all-reduce.2.cloned.1.call-start
  42.9 84.2 %all-gather.2.cloned.1.call-done = bf16[16,512,8,128]{3,2,1,0:T(8,128)(2,1)} async-done(((bf16[1,512,8,128]{3,2,1,0:T(8,128)(2,1)}), bf16[16,512,8,128]{3,2,1,0:T(8,128)(2,1)}) %all-gather.2.cloned.1.call-update) | async-done | bytes 16777232 | tf_op jit(solution)/shard_map/all_gather | solution.py:40
  127.0 13.0 %gather_fusion.5 = bf16[16,512,8,128]{3,2,1,0:T(8,128)(2,1)} fusion(bf16[16,512,8,128]{3,2,1,0:T(8,128)(2,1)} %all-gather.2.cloned.1.call-done, s32[1024]{0:T(1024)S(1)} %pad_clamp_fusion), kind=kCustom, calls=%fused_computation.3.clone | custom fusion | bytes 33554496 | tf_op jit(solution)/shard_map/jit(_take)/gather | solution.py:43
  140.0 14.2 %broadcast_select_fusion = bf16[16,512,8,128]{3,2,1,0:T(8,128)(2,1)} fusion(bf16[16,512,8,128]{3,2,1,0:T(8,128)(2,1)} %gather_fusion.5, pred[16]{0:T(512)(128)(4,1)S(1)} %compare_and_fusion.1), kind=kLoop, calls=%fused_computation.9 | loop fusion | flops 8388608 | bytes 33554448 | tf_op jit(solution)/shard_map/jit(_take)/select_n | solution.py:43
  154.2 25.3 %reshape.130 = bf16[16,512,1024]{2,1,0:T(8,128)(2,1)} reshape(bf16[16,512,8,128]{3,2,1,0:T(8,128)(2,1)} %broadcast_select_fusion) | data formatting | bytes 33554432 | tf_op jit(solution)/shard_map/reshape | solution.py:59
  179.5 17.0 %convolution_convert_fusion = bf16[16,512,1024]{2,1,0:T(8,128)(2,1)} fusion(bf16[16,512,512]{2,1,0:T(8,128)(2,1)} %bitcast.12, bf16[16,512,1024]{2,1,0:T(8,128)(2,1)} %reshape.130), kind=kOutput, calls=%fused_computation.11 | convolution fusion | flops 8598323200 | bytes 41943040 | tf_op jit(solution)/shard_map/spq,sqc->spc/dot_general | solution.py:62
  196.4 25.3 %reshape.131 = bf16[16,4096,128]{2,1,0:T(8,128)(2,1)} reshape(bf16[16,512,1024]{2,1,0:T(8,128)(2,1)} %convolution_convert_fusion) | data formatting | bytes 33554432 | tf_op jit(solution)/shard_map/reshape | solution.py:71
  221.7 13.0 %gather_fusion.4 = bf16[16,512,8,128]{3,2,1,0:T(8,128)(2,1)} fusion(bf16[16,512,8,128]{3,2,1,0:T(8,128)(2,1)} %all-gather.2.cloned.1.call-done, s32[1024]{0:T(1024)S(1)} %pad_clamp_fusion.2), kind=kCustom, calls=%fused_computation.1.clone | custom fusion | bytes 33554496 | tf_op jit(solution)/shard_map/jit(_take)/gather | solution.py:43
  234.7 16.3 %fusion.5 = f32[1,128,128]{2,1,0:T(8,128)} fusion(bf16[16,4096,128]{2,1,0:T(8,128)(2,1)} %reshape.131, bf16[16,512,8,128]{3,2,1,0:T(8,128)(2,1)} %gather_fusion.4, pred[16]{0:T(512)(128)(4,1)S(1)} %compare_and_fusion.2), kind=kOutput, calls=%fused_computation.15 | convolution fusion | flops 2155872256 | bytes 33619984 | tf_op jit(solution)/shard_map/sri,srj->ij/dot_general | solution.py:68
  251.0 80.2 %all-reduce.2.cloned.1.call-done = f32[1,128,128]{2,1,0:T(8,128)} async-done(((f32[1,128,128]{2,1,0:T(8,128)}), f32[1,128,128]{2,1,0:T(8,128)}) %all-reduce.2.cloned.1.call-update) | async-done | bytes 65552 | tf_op jit(solution)/shard_map/psum | solution.py:74
  331.2 1.5 copy.35
  (31 shorter events, 0.7 us)
Async XLA Ops:
  6.5 8.7 %copy-start = (s32[7]{0:T(128)S(1)}, s32[7]{0:T(128)}, u32[]{:S(2)}) copy-start(s32[7]{0:T(128)} %param.17) | copy-start | bytes 88
  6.5 120.5 %all-gather.2.cloned.1.call-start = ((), (), s32[]{:S(2)}) async-start(), calls=%async_computation.2 | async-start | bytes 17825792 | tf_op jit(solution)/shard_map/all_gather | solution.py:40
  18.2 19.1 %all-to-all-start = ((s32[8,2,3]{2,1,0:T(2,128)}), s32[8,2,3]{2,1,0:T(2,128)S(1)}, u32[]{:S(2)}, u32[]{:S(2)}) async-start(s32[8,2,3]{2,1,0:T(2,128)} %copy.24), calls=%async_computation | async-start | bytes 16384 | tf_op jit(solution)/shard_map/all_to_all | solution.py:53
  37.4 142.1 %all-to-all-start.1 = ((bf16[8,2,512,512]{3,2,1,0:T(8,128)(2,1)}), bf16[8,2,512,512]{3,2,1,0:T(8,128)(2,1)}, u32[]{:S(2)}, u32[]{:S(2)}) async-start(bf16[8,2,512,512]{3,2,1,0:T(8,128)(2,1)} %select_multiply_fusion), calls=%async_computation.1 | async-start | bytes 16777216 | tf_op jit(solution)/shard_map/all_to_all | solution.py:46
  42.3 288.9 %all-reduce.2.cloned.1.call-start = ((), (), s32[]{:S(2)}) async-start(), calls=%async_computation.3 | async-start | bytes 131072 | tf_op jit(solution)/shard_map/psum | solution.py:74
  221.7 111.0 %copy-start.1 = (s32[7]{0:T(128)S(1)}, s32[7]{0:T(128)}, u32[]{:S(2)}) copy-start(s32[7]{0:T(128)} %param.17) | copy-start | bytes 88
Sparse Core Ops, SparseCore 0:
  13.0 113.9 all-gather.1
  251.1 80.0 all-reduce.1
where the time goes:
time: 341 us; the launch traced here: 340 us
  waiting for transfers between devices  164 us (48%)
  local copies, waits for them, and re-layouts  90.9 us (27%)
  matrix products  33.3 us (10%)
  other arithmetic  27.7 us (8%)
  between operations  13.5 us (4%)
  starting transfers between devices  9.74 us (3%)
    all_gather x1, waiting for transfers between devices, shards(): lax.all_gather(form_pairs(panel_orbs, occ_rows), 'grp', axis=0, tiled=True)  84.2 us
    psum x1, waiting for transfers between devices, shards(): sigma = lax.psum(partial_sigma, 'grp')  80.2 us
    gather x2, local copies, waits for them, and re-layouts, select_pairs(): return jnp.take(gathered, indices, axis=0)  25.9 us
    reshape x1, local copies, waits for them, and re-layouts, shards(): select_pairs(arrived[:, 1])  25.3 us
    reshape x1, local copies, waits for them, and re-layouts, shards(): screened.reshape(slot_count, grid_points * occ_count, panel_width)  25.3 us
    dot_general x1, matrix products, shards(): jnp.einsum('spq,sqc->spc', incoming, col_pairs, preferred_element_type=jn...  17 us
    dot_general x1, matrix products, shards(): jnp.einsum('sri,srj->ij', row_pairs, screened.reshape(slot_count, grid_po...  16.3 us
    select_n x3, other arithmetic, select_pairs(): return jnp.take(gathered, indices, axis=0)  14.2 us
  transfers between devices with their start and end apart: 4, of which 2 were waited for; matrix products, arithmetic and copies ran while one was open for 21% of the time, Pallas kernels for 0%

commit v1 on v0

--- a/solution.py
+++ b/solution.py
@@ -71,7 +71,7 @@
         screened.reshape(slot_count, grid_points * occ_count, panel_width),
         preferred_element_type=jnp.float32,
     )
-    sigma = lax.psum(partial_sigma, "grp")
+    sigma = jnp.sum(lax.all_gather(partial_sigma, "grp"), axis=0)
     return sigma[None]
 
 

time: 341 us -> 304 us (0.89)
  waiting for transfers between devices: 164 us -> 126 us
    psum x1 -> x0, waiting for transfers between devices: 80.2 us -> none  [shards(): sigma = lax.psum(partial_sigma, 'grp')]
    all_gather x0 -> x1, waiting for transfers between devices: none -> 42.1 us  [shards(): sigma = jnp.sum(lax.all_gather(partial_sigma, 'grp'), axis=0)]
  transfers between devices with their start and end apart: 4 -> 4, of which waited for: 2 -> 2; matrix products, arithmetic and copies ran while one was open for 21% -> 24% of each run, Pallas kernels for 0% -> 0%
where the time goes in v1:
time: 304 us; the launch traced here: 302 us
  waiting for transfers between devices  126 us (41%)
  local copies, waits for them, and re-layouts  89.4 us (29%)
  matrix products  33.3 us (11%)
  other arithmetic  29.6 us (10%)
  between operations  13.5 us (4%)
  starting transfers between devices  9.74 us (3%)
    all_gather x1, waiting for transfers between devices, shards(): lax.all_gather(form_pairs(panel_orbs, occ_rows), 'grp', axis=0, tiled=True)  84.2 us
    all_gather x1, waiting for transfers between devices, shards(): sigma = jnp.sum(lax.all_gather(partial_sigma, 'grp'), axis=0)  42.1 us
    gather x2, local copies, waits for them, and re-layouts, select_pairs(): return jnp.take(gathered, indices, axis=0)  25.9 us
    reshape x1, local copies, waits for them, and re-layouts, shards(): select_pairs(arrived[:, 1])  25.3 us
    reshape x1, local copies, waits for them, and re-layouts, shards(): screened.reshape(slot_count, grid_points * occ_count, panel_width)  25.3 us
    dot_general x1, matrix products, shards(): jnp.einsum('spq,sqc->spc', incoming, col_pairs, preferred_element_type=jn...  17 us
    dot_general x1, matrix products, shards(): jnp.einsum('sri,srj->ij', row_pairs, screened.reshape(slot_count, grid_po...  16.3 us
    select_n x3, other arithmetic, select_pairs(): return jnp.take(gathered, indices, axis=0)  14.2 us
  transfers between devices with their start and end apart: 4, of which 2 were waited for; matrix products, arithmetic and copies ran while one was open for 24% of the time, Pallas kernels for 0%

profile of v1, /device:TPU:0, one launch (start us, length us, event | category | flops | bytes accessed | tf_op | source)
XLA Modules:
  0.0 301.9 jit_solution(16967984671913627495)
XLA Ops:
  6.5 0.7 compare_and_fusion.4
  7.2 0.7 compare_select_fusion.5
  7.9 0.7 convert_bitcast_fusion.1
  8.6 0.1 copy.28
  8.7 1.5 copy.26
  10.2 0.8 gather_fusion
  11.1 0.1 convert_bitcast_fusion
  11.2 0.1 copy.27
  11.3 1.6 multiply_convert_fusion
  12.9 0.7 fusion.8
  13.6 0.8 select_reduce_fusion.1
  14.5 0.7 multiply_add_fusion
  15.1 0.1 convert_reduce_fusion
  15.2 0.7 gather_fusion.3
  15.9 1.3 gather_fusion.2
  17.5 0.7 copy.24
  18.2 4.6 %all-to-all-start = ((s32[8,2,3]{2,1,0:T(2,128)}), s32[8,2,3]{2,1,0:T(2,128)S(1)}, u32[]{:S(2)}, u32[]{:S(2)}) async-start(s32[8,2,3]{2,1,0:T(2,128)} %copy.24), calls=%async_computation | async-start | bytes 16384 | tf_op jit(solution)/shard_map/all_to_all | solution.py:53
  22.9 0.1 convert_element_type.65
  23.0 6.9 %gather_fusion.1 = bf16[16,512,512]{2,1,0:T(8,128)(2,1)} fusion(bf16[7,512,512]{2,1,0:T(8,128)(2,1)} %param.14, s32[1024]{0:T(1024)S(1)} %pad_clamp_fusion.1), kind=kCustom, calls=%fused_computation.5 | custom fusion | bytes 16777280 | tf_op jit(solution)/shard_map/jit(_take)/gather | solution.py:36
  29.9 7.4 %select_multiply_fusion = bf16[8,2,512,512]{3,2,1,0:T(8,128)(2,1)} fusion(bf16[8,2,512,512]{3,2,1,0:T(8,128)(2,1)} %bitcast.41, pred[8,2]{1,0:T(8,128)(4,1)S(1)} %compare_and_fusion, bf16[8,2]{1,0:T(8,128)(2,1)S(1)} %convert_element_type.65), kind=kLoop, calls=%fused_computation.13 | loop fusion | flops 8388608 | bytes 16777264 | tf_op jit(solution)/shard_map/mul | solution.py:36
  37.4 5.0 %all-to-all-start.1 = ((bf16[8,2,512,512]{3,2,1,0:T(8,128)(2,1)}), bf16[8,2,512,512]{3,2,1,0:T(8,128)(2,1)}, u32[]{:S(2)}, u32[]{:S(2)}) async-start(bf16[8,2,512,512]{3,2,1,0:T(8,128)(2,1)} %select_multiply_fusion), calls=%async_computation.1 | async-start | bytes 16777216 | tf_op jit(solution)/shard_map/all_to_all | solution.py:46
  42.3 0.2 all-gather.6.cloned.1.call-start
  42.9 84.2 %all-gather.4.cloned.1.call-done = bf16[16,512,8,128]{3,2,1,0:T(8,128)(2,1)} async-done(((bf16[1,512,8,128]{3,2,1,0:T(8,128)(2,1)}), bf16[16,512,8,128]{3,2,1,0:T(8,128)(2,1)}) %all-gather.4.cloned.1.call-update) | async-done | bytes 16777232 | tf_op jit(solution)/shard_map/all_gather | solution.py:40
  127.0 13.0 %gather_fusion.5 = bf16[16,512,8,128]{3,2,1,0:T(8,128)(2,1)} fusion(bf16[16,512,8,128]{3,2,1,0:T(8,128)(2,1)} %all-gather.4.cloned.1.call-done, s32[1024]{0:T(1024)S(1)} %pad_clamp_fusion), kind=kCustom, calls=%fused_computation.3.clone | custom fusion | bytes 33554496 | tf_op jit(solution)/shard_map/jit(_take)/gather | solution.py:43
  140.0 14.2 %broadcast_select_fusion = bf16[16,512,8,128]{3,2,1,0:T(8,128)(2,1)} fusion(bf16[16,512,8,128]{3,2,1,0:T(8,128)(2,1)} %gather_fusion.5, pred[16]{0:T(512)(128)(4,1)S(1)} %compare_and_fusion.1), kind=kLoop, calls=%fused_computation.9 | loop fusion | flops 8388608 | bytes 33554448 | tf_op jit(solution)/shard_map/jit(_take)/select_n | solution.py:43
  154.2 25.3 %reshape.130 = bf16[16,512,1024]{2,1,0:T(8,128)(2,1)} reshape(bf16[16,512,8,128]{3,2,1,0:T(8,128)(2,1)} %broadcast_select_fusion) | data formatting | bytes 33554432 | tf_op jit(solution)/shard_map/reshape | solution.py:59
  179.5 17.0 %convolution_convert_fusion = bf16[16,512,1024]{2,1,0:T(8,128)(2,1)} fusion(bf16[16,512,512]{2,1,0:T(8,128)(2,1)} %bitcast.12, bf16[16,512,1024]{2,1,0:T(8,128)(2,1)} %reshape.130), kind=kOutput, calls=%fused_computation.11 | convolution fusion | flops 8598323200 | bytes 41943040 | tf_op jit(solution)/shard_map/spq,sqc->spc/dot_general | solution.py:62
  196.4 25.3 %reshape.131 = bf16[16,4096,128]{2,1,0:T(8,128)(2,1)} reshape(bf16[16,512,1024]{2,1,0:T(8,128)(2,1)} %convolution_convert_fusion) | data formatting | bytes 33554432 | tf_op jit(solution)/shard_map/reshape | solution.py:71
  221.7 13.0 %gather_fusion.4 = bf16[16,512,8,128]{3,2,1,0:T(8,128)(2,1)} fusion(bf16[16,512,8,128]{3,2,1,0:T(8,128)(2,1)} %all-gather.4.cloned.1.call-done, s32[1024]{0:T(1024)S(1)} %pad_clamp_fusion.2), kind=kCustom, calls=%fused_computation.1.clone | custom fusion | bytes 33554496 | tf_op jit(solution)/shard_map/jit(_take)/gather | solution.py:43
  234.7 16.3 %fusion.5 = f32[128,128]{1,0:T(8,128)} fusion(bf16[16,4096,128]{2,1,0:T(8,128)(2,1)} %reshape.131, bf16[16,512,8,128]{3,2,1,0:T(8,128)(2,1)} %gather_fusion.4, pred[16]{0:T(512)(128)(4,1)S(1)} %compare_and_fusion.2), kind=kOutput, calls=%fused_computation.15 | convolution fusion | flops 2155872256 | bytes 33619984 | tf_op jit(solution)/shard_map/sri,srj->ij/dot_general | solution.py:68
  251.0 42.1 %all-gather.6.cloned.1.call-done = f32[2048,128]{1,0:T(8,128)} async-done(((f32[128,128]{1,0:T(8,128)}), f32[2048,128]{1,0:T(8,128)}) %all-gather.6.cloned.1.call-update) | async-done | bytes 1048592 | tf_op jit(solution)/shard_map/all_gather | solution.py:74
  293.1 1.9 reduce_sum.45
  (31 shorter events, 0.7 us)
Async XLA Ops:
  6.5 8.7 %copy-start = (s32[7]{0:T(128)S(1)}, s32[7]{0:T(128)}, u32[]{:S(2)}) copy-start(s32[7]{0:T(128)} %param.17) | copy-start | bytes 88
  6.5 120.5 %all-gather.4.cloned.1.call-start = ((), (), s32[]{:S(2)}) async-start(), calls=%async_computation.2 | async-start | bytes 17825792 | tf_op jit(solution)/shard_map/all_gather | solution.py:40
  18.2 19.1 %all-to-all-start = ((s32[8,2,3]{2,1,0:T(2,128)}), s32[8,2,3]{2,1,0:T(2,128)S(1)}, u32[]{:S(2)}, u32[]{:S(2)}) async-start(s32[8,2,3]{2,1,0:T(2,128)} %copy.24), calls=%async_computation | async-start | bytes 16384 | tf_op jit(solution)/shard_map/all_to_all | solution.py:53
  37.4 142.1 %all-to-all-start.1 = ((bf16[8,2,512,512]{3,2,1,0:T(8,128)(2,1)}), bf16[8,2,512,512]{3,2,1,0:T(8,128)(2,1)}, u32[]{:S(2)}, u32[]{:S(2)}) async-start(bf16[8,2,512,512]{3,2,1,0:T(8,128)(2,1)} %select_multiply_fusion), calls=%async_computation.1 | async-start | bytes 16777216 | tf_op jit(solution)/shard_map/all_to_all | solution.py:46
  42.3 250.8 %all-gather.6.cloned.1.call-start = ((), (), s32[]{:S(2)}) async-start(), calls=%async_computation.3 | async-start | bytes 1114112 | tf_op jit(solution)/shard_map/all_gather | solution.py:74
  221.7 73.3 %copy-start.1 = (s32[7]{0:T(128)S(1)}, s32[7]{0:T(128)}, u32[]{:S(2)}) copy-start(s32[7]{0:T(128)} %param.17) | copy-start | bytes 88
Sparse Core Ops, SparseCore 0:
  13.0 113.9 all-gather.3
  251.1 41.9 all-gather.5
